TPU v7x, 256 devices: a whole 4x4x8 slice. The times are simulated.
256 devices in a mesh: col: 16 (over z, core), row: 16 (over x, y).
Axes of the slice: x: 4, y: 4, z: 8, core: 2. Of those that a mesh axis runs over, the one named last changes fastest.
Arguments:
- lower_cols: float32 [4096, 2048], P('col', 'row'), may hold values from -6 to 6
- pivot_rows: float32 [8192, 4096], P('row', 'col')
- pattern: int32 [64, 32], replicated, may hold values 0 or 1
- panel_in: float32 [8192, 2048], P('col', 'row'), may hold values from -6 to 6
- diag_in: float32 [64, 128, 128], P('col'), as said below
Outputs:
- panel: float32 [8192, 2048], P('col', 'row')
- factor: float32 [64, 128, 128], P('col')
Inputs may be any that keep to these rules, and one draw needn't show every extreme that they name: diag_in holds symmetric blocks with diagonal entries between 2.5 and 4.5; diag_in[j] - dsum[j] is positive definite.
All inputs are finite; a program needn't handle non-finite values.
Results may differ from a plain program's by a relative error of at most 0.00005.
Values sent between devices are 32-bit elements; how exact they have to be, the bound alone decides.
A program may use at most 128 MiB of HBM per device.

v0:
```python
import jax
import jax.numpy as jnp
from jax import lax
from jax.sharding import PartitionSpec as P

B = 128


def shards(lower_cols, pivot_rows, pattern, panel_in, diag_in):
    col_index = lax.axis_index("col")
    k_local = lower_cols.shape[0] // B
    targets = pattern.shape[0]
    own_targets = diag_in.shape[0]
    width = panel_in.shape[1]
    whole_pivot = lax.all_gather(pivot_rows, "row", axis=0, tiled=True)
    local_pattern = lax.dynamic_slice_in_dim(pattern, col_index * k_local, k_local, 1).astype(
        jnp.float32
    )
    masked = whole_pivot.reshape(targets, B, k_local, B) * local_pattern[:, None, :, None]
    masked = masked.reshape(targets * B, k_local * B)
    update = lax.psum_scatter(
        jnp.dot(
            masked, lower_cols, precision=lax.Precision.HIGHEST, preferred_element_type=jnp.float32
        ),
        "col",
        scatter_dimension=0,
        tiled=True,
    )
    blocks = masked.reshape(targets, B, k_local * B)
    partial_diag = jnp.einsum("jak,jbk->jab", blocks, blocks, precision=lax.Precision.HIGHEST)
    dsum = lax.psum_scatter(partial_diag, "col", scatter_dimension=0, tiled=True)
    factor = jnp.linalg.cholesky(diag_in - dsum)
    residue = (panel_in - update).reshape(own_targets, B, width)
    solved = lax.linalg.triangular_solve(factor, residue, left_side=True, lower=True)
    return (solved.reshape(own_targets * B, width), factor)


def solution(mesh):
    in_specs = (P("col", "row"), P("row", "col"), P(), P("col", "row"), P("col", None, None))
    out_specs = (P("col", "row"), P("col", None, None))
    return jax.shard_map(shards, mesh=mesh, in_specs=in_specs, out_specs=out_specs, check_vma=False)
```

profile of v0, /device:TPU:2, one launch (start us, length us, event | category | flops | bytes accessed | tf_op | source)
XLA Modules:
  0.0 266.4 jit_solution(10246708308004626296)
XLA Ops:
  7.2 0.0 copy-start
  7.2 0.0 all-gather.2.cloned.1.call-start
  7.2 0.7 all-gather.2.cloned.1.call-update
  7.9 0.0 reduce-scatter.3.cloned.1.call-start
  8.0 0.7 dynamic-slice_convert_fusion
  8.7 0.1 copy.13
  8.8 0.1 mul.24
  8.9 80.3 %all-gather.2.cloned.1.call-done = f32[8192,256]{1,0:T(8,128)} async-done(((f32[512,256]{1,0:T(8,128)}), f32[8192,256]{1,0:T(8,128)}) %all-gather.2.cloned.1.call-update) | async-done | bytes 8388624 | tf_op jit(solution)/shard_map/all_gather | solution.py:15
  89.2 16.6 %fusion.2 = f32[64,128,128]{1,2,0:T(8,128)} fusion(f32[64,128,256]{2,1,0:T(8,128)} %bitcast.23, f32[64,256]{1,0:T(8,128)S(1)} %bitcast.26), kind=kOutput, calls=%fused_computation.3 | convolution fusion | flops 3223322624 | bytes 12648448 | tf_op jit(solution)/shard_map/jak,jbk->jab/dot_general | solution.py:30
  105.8 0.0 reduce-scatter.3.cloned.1.call-update
  105.9 0.0 reduce-scatter.5.cloned.1.call-start
  105.9 5.4 %mul.28 = f32[64,128,2,128]{3,2,1,0:T(2,128)} broadcast(f32[64,2]{1,0:T(8,128)S(1)} %copy.13), dimensions={0,2} | broadcast | bytes 8389120 | tf_op jit(solution)/shard_map/mul | solution.py:19
  111.3 0.0 copy-done
  111.3 0.0 copy-start.2
  111.3 0.0 copy-start.1
  111.3 12.2 %fusion = f32[8192,128]{1,0:T(8,128)} fusion(f32[256,128]{1,0:T(8,128)S(1)} %copy-done, f32[8192,256]{1,0:T(8,128)} %all-gather.2.cloned.1.call-done, f32[1024,8,2,128]{3,2,1,0:T(2,128)} %bitcast.24), kind=kOutput, calls=%fused_computation.1 | convolution fusion | flops 3223322624 | bytes 21102592 | tf_op jit(solution)/shard_map/dot_general | solution.py:22
  123.5 0.0 reduce-scatter.5.cloned.1.call-update
  123.6 0.0 copy-done.2
  123.6 0.1 copy.15
  123.8 45.4 %reduce-scatter.3.cloned.1.call-done = f32[4,128,128]{1,2,0:T(8,128)} async-done(((f32[64,128,128]{1,2,0:T(8,128)}), f32[4,128,128]{1,2,0:T(8,128)}) %reduce-scatter.3.cloned.1.call-update) | async-done | bytes 262160 | tf_op jit(solution)/shard_map/reduce_scatter | solution.py:31
  169.2 1.0 sub.6
  170.2 0.1 copy.16
  170.3 46.9 %custom-call.7 = f32[4,128,128]{2,1,0:T(8,128)S(1)} custom-call(f32[4,128,128]{2,1,0:T(8,128)S(1)} %fusion.7), custom_call_target="Cholesky" | custom-call | tf_op jit(solution)/shard_map/jit(cholesky)/cholesky | solution.py:32
  217.3 0.1 compare_reduce_fusion
  217.4 0.8 select_bitcast_fusion
  218.2 39.3 %custom-call.8 = f32[4,1,128,128]{2,3,1,0:T(8,128)S(1)} custom-call(f32[4,1,128,128]{3,2,1,0:T(8,128)S(1)} %get-tuple-element.2), custom_call_target="InvertDiagBlocksLowerTriangular" | custom-call | tf_op jit(solution)/shard_map/triangular_solve | solution.py:34
  257.5 0.0 reduce-scatter.5.cloned.1.call-done
  257.5 0.0 copy-done.1
  257.6 1.0 sub.7
  258.5 1.3 fusion.5
  (5 shorter events, 0.1 us)
Async XLA Ops:
  7.2 104.2 %copy-start = (f32[256,128]{1,0:T(8,128)S(1)}, f32[256,128]{1,0:T(8,128)}, u32[]{:S(2)}) copy-start(f32[256,128]{1,0:T(8,128)} %param.5) | copy-start | bytes 393220
  7.2 82.0 %all-gather.2.cloned.1.call-start = ((), (), s32[]{:S(2)}) async-start(), calls=%async_computation.2 | async-start | bytes 8912896 | tf_op jit(solution)/shard_map/all_gather | solution.py:15
  7.9 161.3 %reduce-scatter.3.cloned.1.call-start = ((), (), s32[]{:S(2)}) async-start(), calls=%async_computation.3 | async-start | bytes 4456448 | tf_op jit(solution)/shard_map/reduce_scatter | solution.py:31
  105.9 151.7 %reduce-scatter.5.cloned.1.call-start = ((), (), s32[]{:S(2)}) async-start(), calls=%async_computation.4 | async-start | bytes 4456448 | tf_op jit(solution)/shard_map/reduce_scatter | solution.py:21
  111.3 12.2 %copy-start.2 = (f32[4,128,128]{2,1,0:T(8,128)S(1)}, f32[4,128,128]{2,1,0:T(8,128)}, u32[]{:S(2)}) copy-start(f32[4,128,128]{2,1,0:T(8,128)} %param.9) | copy-start | bytes 786436
  111.3 146.2 %copy-start.1 = (f32[512,128]{1,0:T(8,128)S(1)}, f32[512,128]{1,0:T(8,128)}, u32[]{:S(2)}) copy-start(f32[512,128]{1,0:T(8,128)} %param.8) | copy-start | bytes 786436
Sparse Core Ops, SparseCore 0:
  10.4 78.7 all-gather.1
  106.0 63.1 reduce-scatter.2
  171.7 62.2 reduce-scatter.4
where the time goes:
time: 267 us; the launch traced here: 266 us
  waiting for transfers between devices  126 us (47%)
  other arithmetic  89.9 us (34%)
  matrix products  30.1 us (11%)
  between operations  13.9 us (5%)
  local copies, waits for them, and re-layouts  5.94 us (2%)
    all_gather x1, waiting for transfers between devices, shards(): whole_pivot = lax.all_gather(pivot_rows, 'row', axis=0, tiled=True)  80.3 us
    another operation x4, other arithmetic, shards(): factor = jnp.linalg.cholesky(diag_in - dsum)  47.1 us
    reduce_scatter x1, waiting for transfers between devices, shards(): lax.psum_scatter(partial_diag, 'col', scatter_dimension=0, tiled=True)  45.4 us
    another operation x3, other arithmetic, shards(): lax.linalg.triangular_solve(factor, residue, left_side=True, lower=True)  40.1 us
    dot_general x1, matrix products, shards(): jnp.einsum('jak,jbk->jab', blocks, blocks, precision=lax.Precision.HIGHEST)  16.6 us
    dot_general x1, matrix products, shards(): jnp.dot(masked, lower_cols, precision=lax.Precision.HIGHEST, preferred_el...  12.2 us
    mul x2, local copies, waits for them, and re-layouts, shards(): whole_pivot.reshape(targets, B, k_local, B)  5.56 us
  transfers between devices with their start and end apart: 3, of which 2 were waited for; matrix products, arithmetic and copies ran while one was open for 40% of the time, Pallas kernels for 0%

commit v1 on v0

--- a/solution.py
+++ b/solution.py
@@ -1,3 +1,4 @@
+import functools
 import jax
 import jax.numpy as jnp
 from jax import lax
@@ -6,13 +7,43 @@
 B = 128
 
 
+def time_tracks(local_array, net_axis):
+    frame_out, now, mixed_arr = (
+        jax.lax.axis_size(net_axis),
+        jax.lax.axis_index(net_axis),
+        local_array.shape[0],
+    )
+    views = tuple(((it, (it + 1) % frame_out) for it in range(frame_out)))
+    windows = tuple(((it, (it - 1) % frame_out) for it in range(frame_out)))
+    low = jnp.zeros(
+        (*local_array.shape[:0], frame_out * mixed_arr, *local_array.shape[1:]), local_array.dtype
+    )
+    low = lax.dynamic_update_slice_in_dim(low, local_array, now * mixed_arr, axis=0)
+    carry = taken_in = local_array
+    h_now = frame_out // 2
+    for ix in range(1, h_now + 1):
+        carry = jax.lax.ppermute(carry, net_axis, views)
+        low = lax.dynamic_update_slice_in_dim(
+            low, carry, (now - ix) % frame_out * mixed_arr, axis=0
+        )
+        if ix < frame_out - h_now:
+            taken_in = jax.lax.ppermute(taken_in, net_axis, perm=windows)
+            low = lax.dynamic_update_slice_in_dim(
+                low, taken_in, (now + ix) % frame_out * mixed_arr, axis=0
+            )
+    return low
+
+
+attach_rows = functools.partial(time_tracks, net_axis="row")
+
+
 def shards(lower_cols, pivot_rows, pattern, panel_in, diag_in):
     col_index = lax.axis_index("col")
     k_local = lower_cols.shape[0] // B
     targets = pattern.shape[0]
     own_targets = diag_in.shape[0]
     width = panel_in.shape[1]
-    whole_pivot = lax.all_gather(pivot_rows, "row", axis=0, tiled=True)
+    whole_pivot = attach_rows(pivot_rows)
     local_pattern = lax.dynamic_slice_in_dim(pattern, col_index * k_local, k_local, 1).astype(
         jnp.float32
     )

time: 267 us -> 300 us (1.12)
  starting transfers between devices: 0.12 us -> 29.1 us
  local copies, waits for them, and re-layouts: 5.94 us -> 28.4 us
  waiting for transfers between devices: 126 us -> 108 us
    all_gather x1 -> x0, waiting for transfers between devices: 80.3 us -> none  [shards(): whole_pivot = lax.all_gather(pivot_rows, 'row', axis=0, tiled=True)]
    ppermute x0 -> x15, waiting for transfers between devices: none -> 55.8 us  [the longest x8 55.7 us: time_tracks(): carry = jax.lax.ppermute(carry, net_axis, views)]
    ppermute x0 -> x15, starting transfers between devices: none -> 29 us  [the longest x7 27.3 us: time_tracks(): taken_in = jax.lax.ppermute(taken_in, net_axis, perm=windows)]
    dynamic_update_slice x0 -> x16, local copies, waits for them, and re-layouts: none -> 18.7 us  [the longest x8 9.91 us: time_tracks(): lax.dynamic_update_slice_in_dim(low, carry, (now - ix) % frame_out * mixe...]
    reduce_scatter x1, waiting for transfers between devices: 45.4 us -> 51.9 us  [shards(): lax.psum_scatter(partial_diag, 'col', scatter_dimension=0, tiled=True)]
    broadcast_in_dim x0 -> x1, local copies, waits for them, and re-layouts: none -> 3.78 us  [time_tracks(): jnp.zeros((*local_array.shape[:0], frame_out * mixed_arr, *local_array.sh...]
  transfers between devices with their start and end apart: 3 -> 17, of which waited for: 2 -> 9; matrix products, arithmetic and copies ran while one was open for 40% -> 43% of each run, Pallas kernels for 0% -> 0%
where the time goes in v1:
time: 300 us
  waiting for transfers between devices  108 us (36%)
  other arithmetic  89.9 us (30%)
  matrix products  30.2 us (10%)
  starting transfers between devices  29.1 us (10%)
  local copies, waits for them, and re-layouts  28.4 us (9%)
  between operations  14.3 us (5%)
    ppermute x8, waiting for transfers between devices, time_tracks(): carry = jax.lax.ppermute(carry, net_axis, views)  55.7 us
    reduce_scatter x1, waiting for transfers between devices, shards(): lax.psum_scatter(partial_diag, 'col', scatter_dimension=0, tiled=True)  51.9 us
    another operation x4, other arithmetic, shards(): factor = jnp.linalg.cholesky(diag_in - dsum)  47.1 us
    another operation x3, other arithmetic, shards(): lax.linalg.triangular_solve(factor, residue, left_side=True, lower=True)  40.1 us
    ppermute x7, starting transfers between devices, time_tracks(): taken_in = jax.lax.ppermute(taken_in, net_axis, perm=windows)  27.3 us
    dot_general x1, matrix products, shards(): jnp.einsum('jak,jbk->jab', blocks, blocks, precision=lax.Precision.HIGHEST)  16.6 us
    dot_general x1, matrix products, shards(): jnp.dot(masked, lower_cols, precision=lax.Precision.HIGHEST, preferred_el...  12.2 us
    dynamic_update_slice x8, local copies, waits for them, and re-layouts, time_tracks(): lax.dynamic_update_slice_in_dim(low, carry, (now - ix) % frame_out * mixe...  9.91 us
  transfers between devices with their start and end apart: 17, of which 9 were waited for; matrix products, arithmetic and copies ran while one was open for 43% of the time, Pallas kernels for 0%

profile of v1, /device:TPU:2, one launch (start us, length us, event | category | flops | bytes accessed | tf_op | source)
XLA Modules:
  0.0 299.5 jit_solution(12884865325463041097)
XLA Ops:
  7.2 1.7 collective-permute-start
  8.9 2.6 collective-permute-start.1
  11.4 11.8 %collective-permute-done = f32[512,256]{1,0:T(8,128)S(1)} collective-permute-done((f32[512,256]{1,0:T(8,128)}, f32[512,256]{1,0:T(8,128)S(1)}, u32[]{:S(2)}, u32[]{:S(2)}) %collective-permute-start) | collective-permute-done | bytes 524320 | tf_op jit(solution)/shard_map/ppermute | solution.py:25
  23.3 4.1 %collective-permute-start.3 = (f32[512,256]{1,0:T(8,128)S(1)}, f32[512,256]{1,0:T(8,128)S(1)}, u32[]{:S(2)}, u32[]{:S(2)}) collective-permute-start(f32[512,256]{1,0:T(8,128)S(1)} %collective-permute-done.1), channel_id=1, source_target_pairs={{0,15},{1,0},{2,1},{3,2},{4,3},{5,4},{6,5},{7,6},{8,7},{9,8},{10,9... | collective-permute-start | bytes 1572872 | tf_op jit(solution)/shard_map/ppermute | solution.py:30
  27.4 10.8 %collective-permute-done.2 = f32[512,256]{1,0:T(8,128)S(1)} collective-permute-done((f32[512,256]{1,0:T(8,128)S(1)}, f32[512,256]{1,0:T(8,128)S(1)}, u32[]{:S(2)}, u32[]{:S(2)}) %collective-permute-start.2) | collective-permute-done | bytes 524320 | tf_op jit(solution)/shard_map/ppermute | solution.py:25
  38.2 4.1 %collective-permute-start.5 = (f32[512,256]{1,0:T(8,128)S(1)}, f32[512,256]{1,0:T(8,128)S(1)}, u32[]{:S(2)}, u32[]{:S(2)}) collective-permute-start(f32[512,256]{1,0:T(8,128)S(1)} %collective-permute-done.3), channel_id=1, source_target_pairs={{0,15},{1,0},{2,1},{3,2},{4,3},{5,4},{6,5},{7,6},{8,7},{9,8},{10,9... | collective-permute-start | bytes 1572872 | tf_op jit(solution)/shard_map/ppermute | solution.py:30
  42.4 9.9 %collective-permute-done.4 = f32[512,256]{1,0:T(8,128)S(1)} collective-permute-done((f32[512,256]{1,0:T(8,128)S(1)}, f32[512,256]{1,0:T(8,128)S(1)}, u32[]{:S(2)}, u32[]{:S(2)}) %collective-permute-start.4) | collective-permute-done | bytes 524320 | tf_op jit(solution)/shard_map/ppermute | solution.py:25
  52.3 4.1 %collective-permute-start.7 = (f32[512,256]{1,0:T(8,128)S(1)}, f32[512,256]{1,0:T(8,128)}, u32[]{:S(2)}, u32[]{:S(2)}) collective-permute-start(f32[512,256]{1,0:T(8,128)S(1)} %collective-permute-done.5), channel_id=1, source_target_pairs={{0,15},{1,0},{2,1},{3,2},{4,3},{5,4},{6,5},{7,6},{8,7},{9,8},{10,9... | collective-permute-start | bytes 1572872 | tf_op jit(solution)/shard_map/ppermute | solution.py:30
  56.4 9.2 %collective-permute-done.6 = f32[512,256]{1,0:T(8,128)} collective-permute-done((f32[512,256]{1,0:T(8,128)S(1)}, f32[512,256]{1,0:T(8,128)}, u32[]{:S(2)}, u32[]{:S(2)}) %collective-permute-start.6) | collective-permute-done | bytes 524320 | tf_op jit(solution)/shard_map/ppermute | solution.py:25
  65.6 4.1 %collective-permute-start.9 = (f32[512,256]{1,0:T(8,128)}, f32[512,256]{1,0:T(8,128)}, u32[]{:S(2)}, u32[]{:S(2)}) collective-permute-start(f32[512,256]{1,0:T(8,128)} %collective-permute-done.7), channel_id=1, source_target_pairs={{0,15},{1,0},{2,1},{3,2},{4,3},{5,4},{6,5},{7,6},{8,7},{9,8},{10,9... | collective-permute-start | bytes 1572872 | tf_op jit(solution)/shard_map/ppermute | solution.py:30
  69.7 3.8 %broadcast_in_dim.8 = f32[8192,256]{1,0:T(8,128)} broadcast(f32[]{:T(128)} %constant.131.clone.1), dimensions={} | broadcast | bytes 8388612 | tf_op jit(solution)/shard_map/broadcast_in_dim | solution.py:18
  74.3 3.9 %collective-permute-done.8 = f32[512,256]{1,0:T(8,128)} collective-permute-done((f32[512,256]{1,0:T(8,128)}, f32[512,256]{1,0:T(8,128)}, u32[]{:S(2)}, u32[]{:S(2)}) %collective-permute-start.8) | collective-permute-done | bytes 524320 | tf_op jit(solution)/shard_map/ppermute | solution.py:25
  81.0 1.9 constant_dynamic-update-slice_fusion.12
  82.8 4.1 %collective-permute-start.11 = (f32[512,256]{1,0:T(8,128)}, f32[512,256]{1,0:T(8,128)S(1)}, u32[]{:S(2)}, u32[]{:S(2)}) collective-permute-start(f32[512,256]{1,0:T(8,128)} %collective-permute-done.9), channel_id=1, source_target_pairs={{0,15},{1,0},{2,1},{3,2},{4,3},{5,4},{6,5},{7,6},{8,7},{9,8},{10,9... | collective-permute-start | bytes 1572872 | tf_op jit(solution)/shard_map/ppermute | solution.py:30
  87.8 2.7 collective-permute-done.10
  92.2 1.9 constant_dynamic-update-slice_fusion.8
  94.1 1.9 constant_dynamic-update-slice_fusion.7
  96.1 4.1 %collective-permute-start.13 = (f32[512,256]{1,0:T(8,128)S(1)}, f32[512,256]{1,0:T(8,128)S(1)}, u32[]{:S(2)}, u32[]{:S(2)}) collective-permute-start(f32[512,256]{1,0:T(8,128)S(1)} %collective-permute-done.11), channel_id=1, source_target_pairs={{0,15},{1,0},{2,1},{3,2},{4,3},{5,4},{6,5},{7,6},{8,7},{9,8},{10,9... | collective-permute-start | bytes 1572872 | tf_op jit(solution)/shard_map/ppermute | solution.py:30
  100.2 1.9 constant_dynamic-update-slice_fusion.6
  102.1 1.3 collective-permute-done.12
  103.4 1.9 constant_dynamic-update-slice_fusion.5
  105.3 0.9 constant_dynamic-update-slice_fusion.4
  108.7 6.0 %collective-permute-done.14 = f32[512,256]{1,0:T(8,128)S(1)} collective-permute-done((f32[512,256]{1,0:T(8,128)S(1)}, f32[512,256]{1,0:T(8,128)S(1)}, u32[]{:S(2)}, u32[]{:S(2)}) %collective-permute-start.14) | collective-permute-done | bytes 524320 | tf_op jit(solution)/shard_map/ppermute | solution.py:25
  115.5 16.6 %fusion.2 = f32[64,128,128]{1,2,0:T(8,128)} fusion(f32[64,128,256]{2,1,0:T(8,128)} %bitcast, f32[64,256]{1,0:T(8,128)S(1)} %bitcast.25), kind=kOutput, calls=%fused_computation.3 | convolution fusion | flops 3223322624 | bytes 12648448 | tf_op jit(solution)/shard_map/jak,jbk->jab/dot_general | solution.py:61
  132.2 5.4 %mul.92 = f32[64,128,2,128]{3,2,1,0:T(2,128)} broadcast(f32[64,2]{1,0:T(8,128)S(1)} %copy.13), dimensions={0,2} | broadcast | bytes 8389120 | tf_op jit(solution)/shard_map/mul | solution.py:50
  137.7 12.2 %fusion = f32[8192,128]{1,0:T(8,128)} fusion(f32[256,128]{1,0:T(8,128)S(1)} %copy-done, f32[8192,256]{1,0:T(8,128)} %constant_dynamic-update-slice_fusion, f32[1024,8,2,128]{3,2,1,0:T(2,128)} %bitcast.23), kind=kOutput, calls=%fused_computation.1 | convolution fusion | flops 3223322624 | bytes 21102592 | tf_op jit(solution)/shard_map/dot_general | solution.py:53
  150.1 51.9 %reduce-scatter.3.cloned.1.call-done = f32[4,128,128]{1,2,0:T(8,128)} async-done(((f32[64,128,128]{1,2,0:T(8,128)}), f32[4,128,128]{1,2,0:T(8,128)}) %reduce-scatter.3.cloned.1.call-update) | async-done | bytes 262160 | tf_op jit(solution)/shard_map/reduce_scatter | solution.py:62
  202.0 1.0 sub.38
  203.2 46.9 %custom-call.7 = f32[4,128,128]{2,1,0:T(8,128)S(1)} custom-call(f32[4,128,128]{2,1,0:T(8,128)S(1)} %fusion.7), custom_call_target="Cholesky" | custom-call | tf_op jit(solution)/shard_map/jit(cholesky)/cholesky | solution.py:63
  251.1 39.3 %custom-call.8 = f32[4,1,128,128]{2,3,1,0:T(8,128)S(1)} custom-call(f32[4,1,128,128]{3,2,1,0:T(8,128)S(1)} %get-tuple-element.2), custom_call_target="InvertDiagBlocksLowerTriangular" | custom-call | tf_op jit(solution)/shard_map/triangular_solve | solution.py:65
  290.4 1.0 sub.39
  291.4 1.3 fusion.5
  (51 shorter events, 10.8 us)
Async XLA Ops:
  7.2 130.5 %copy-start = (f32[256,128]{1,0:T(8,128)S(1)}, f32[256,128]{1,0:T(8,128)}, u32[]{:S(2)}) copy-start(f32[256,128]{1,0:T(8,128)} %param.5) | copy-start | bytes 393220
  7.2 66.3 %copy-start.1 = (f32[512,256]{1,0:T(8,128)S(1)}, f32[512,256]{1,0:T(8,128)}, u32[]{:S(2)}) copy-start(f32[512,256]{1,0:T(8,128)} %param.6) | copy-start | bytes 1572868
  7.2 194.8 %reduce-scatter.3.cloned.1.call-start = ((), (), s32[]{:S(2)}) async-start(), calls=%async_computation.2 | async-start | bytes 4456448 | tf_op jit(solution)/shard_map/reduce_scatter | solution.py:62
  7.2 16.1 %collective-permute-start = (f32[512,256]{1,0:T(8,128)}, f32[512,256]{1,0:T(8,128)S(1)}, u32[]{:S(2)}, u32[]{:S(2)}) collective-permute-start(f32[512,256]{1,0:T(8,128)} %param.6), channel_id=1, source_target_pairs={{0,1},{1,2},{2,3},{3,4},{4,5},{5,6},{6,7},{7,8},{8,9},{9,10},{10,1... | collective-permute-start | bytes 1572872 | tf_op jit(solution)/shard_map/ppermute | solution.py:25
  8.9 14.4 %collective-permute-start.1 = (f32[512,256]{1,0:T(8,128)}, f32[512,256]{1,0:T(8,128)S(1)}, u32[]{:S(2)}, u32[]{:S(2)}) collective-permute-start(f32[512,256]{1,0:T(8,128)} %param.6), channel_id=1, source_target_pairs={{0,15},{1,0},{2,1},{3,2},{4,3},{5,4},{6,5},{7,6},{8,7},{9,8},{10,9... | collective-permute-start | bytes 1572872 | tf_op jit(solution)/shard_map/ppermute | solution.py:30
  23.3 14.9 %collective-permute-start.2 = (f32[512,256]{1,0:T(8,128)S(1)}, f32[512,256]{1,0:T(8,128)S(1)}, u32[]{:S(2)}, u32[]{:S(2)}) collective-permute-start(f32[512,256]{1,0:T(8,128)S(1)} %collective-permute-done), channel_id=1, source_target_pairs={{0,1},{1,2},{2,3},{3,4},{4,5},{5,6},{6,7},{7,8},{8,9},{9,10},{10,1... | collective-permute-start | bytes 1572872 | tf_op jit(solution)/shard_map/ppermute | solution.py:25
  23.3 14.9 %collective-permute-start.3 = (f32[512,256]{1,0:T(8,128)S(1)}, f32[512,256]{1,0:T(8,128)S(1)}, u32[]{:S(2)}, u32[]{:S(2)}) collective-permute-start(f32[512,256]{1,0:T(8,128)S(1)} %collective-permute-done.1), channel_id=1, source_target_pairs={{0,15},{1,0},{2,1},{3,2},{4,3},{5,4},{6,5},{7,6},{8,7},{9,8},{10,9... | collective-permute-start | bytes 1572872 | tf_op jit(solution)/shard_map/ppermute | solution.py:30
  38.2 27.4 %copy-start.2 = (f32[512,256]{1,0:T(8,128)}, f32[512,256]{1,0:T(8,128)S(1)}, u32[]{:S(2)}) copy-start(f32[512,256]{1,0:T(8,128)S(1)} %collective-permute-done.2) | copy-start | bytes 1572868
  38.2 14.1 %collective-permute-start.4 = (f32[512,256]{1,0:T(8,128)S(1)}, f32[512,256]{1,0:T(8,128)S(1)}, u32[]{:S(2)}, u32[]{:S(2)}) collective-permute-start(f32[512,256]{1,0:T(8,128)S(1)} %collective-permute-done.2), channel_id=1, source_target_pairs={{0,1},{1,2},{2,3},{3,4},{4,5},{5,6},{6,7},{7,8},{8,9},{9,10},{10,1... | collective-permute-start | bytes 1572872 | tf_op jit(solution)/shard_map/ppermute | solution.py:25
  38.2 14.1 %collective-permute-start.5 = (f32[512,256]{1,0:T(8,128)S(1)}, f32[512,256]{1,0:T(8,128)S(1)}, u32[]{:S(2)}, u32[]{:S(2)}) collective-permute-start(f32[512,256]{1,0:T(8,128)S(1)} %collective-permute-done.3), channel_id=1, source_target_pairs={{0,15},{1,0},{2,1},{3,2},{4,3},{5,4},{6,5},{7,6},{8,7},{9,8},{10,9... | collective-permute-start | bytes 1572872 | tf_op jit(solution)/shard_map/ppermute | solution.py:30
  52.3 13.3 %collective-permute-start.6 = (f32[512,256]{1,0:T(8,128)S(1)}, f32[512,256]{1,0:T(8,128)}, u32[]{:S(2)}, u32[]{:S(2)}) collective-permute-start(f32[512,256]{1,0:T(8,128)S(1)} %collective-permute-done.4), channel_id=1, source_target_pairs={{0,1},{1,2},{2,3},{3,4},{4,5},{5,6},{6,7},{7,8},{8,9},{9,10},{10,1... | collective-permute-start | bytes 1572872 | tf_op jit(solution)/shard_map/ppermute | solution.py:25
  52.3 13.3 %collective-permute-start.7 = (f32[512,256]{1,0:T(8,128)S(1)}, f32[512,256]{1,0:T(8,128)}, u32[]{:S(2)}, u32[]{:S(2)}) collective-permute-start(f32[512,256]{1,0:T(8,128)S(1)} %collective-permute-done.5), channel_id=1, source_target_pairs={{0,15},{1,0},{2,1},{3,2},{4,3},{5,4},{6,5},{7,6},{8,7},{9,8},{10,9... | collective-permute-start | bytes 1572872 | tf_op jit(solution)/shard_map/ppermute | solution.py:30
  65.6 12.7 %collective-permute-start.8 = (f32[512,256]{1,0:T(8,128)}, f32[512,256]{1,0:T(8,128)}, u32[]{:S(2)}, u32[]{:S(2)}) collective-permute-start(f32[512,256]{1,0:T(8,128)} %collective-permute-done.6), channel_id=1, source_target_pairs={{0,1},{1,2},{2,3},{3,4},{4,5},{5,6},{6,7},{7,8},{8,9},{9,10},{10,1... | collective-permute-start | bytes 1572872 | tf_op jit(solution)/shard_map/ppermute | solution.py:25
  65.6 17.2 %collective-permute-start.9 = (f32[512,256]{1,0:T(8,128)}, f32[512,256]{1,0:T(8,128)}, u32[]{:S(2)}, u32[]{:S(2)}) collective-permute-start(f32[512,256]{1,0:T(8,128)} %collective-permute-done.7), channel_id=1, source_target_pairs={{0,15},{1,0},{2,1},{3,2},{4,3},{5,4},{6,5},{7,6},{8,7},{9,8},{10,9... | collective-permute-start | bytes 1572872 | tf_op jit(solution)/shard_map/ppermute | solution.py:30
  78.3 12.3 %collective-permute-start.10 = (f32[512,256]{1,0:T(8,128)}, f32[512,256]{1,0:T(8,128)S(1)}, u32[]{:S(2)}, u32[]{:S(2)}) collective-permute-start(f32[512,256]{1,0:T(8,128)} %collective-permute-done.8), channel_id=1, source_target_pairs={{0,1},{1,2},{2,3},{3,4},{4,5},{5,6},{6,7},{7,8},{8,9},{9,10},{10,1... | collective-permute-start | bytes 1572872 | tf_op jit(solution)/shard_map/ppermute | solution.py:25
  82.8 13.2 %collective-permute-start.11 = (f32[512,256]{1,0:T(8,128)}, f32[512,256]{1,0:T(8,128)S(1)}, u32[]{:S(2)}, u32[]{:S(2)}) collective-permute-start(f32[512,256]{1,0:T(8,128)} %collective-permute-done.9), channel_id=1, source_target_pairs={{0,15},{1,0},{2,1},{3,2},{4,3},{5,4},{6,5},{7,6},{8,7},{9,8},{10,9... | collective-permute-start | bytes 1572872 | tf_op jit(solution)/shard_map/ppermute | solution.py:30
  90.6 12.8 %collective-permute-start.12 = (f32[512,256]{1,0:T(8,128)S(1)}, f32[512,256]{1,0:T(8,128)S(1)}, u32[]{:S(2)}, u32[]{:S(2)}) collective-permute-start(f32[512,256]{1,0:T(8,128)S(1)} %collective-permute-done.10), channel_id=1, source_target_pairs={{0,1},{1,2},{2,3},{3,4},{4,5},{5,6},{6,7},{7,8},{8,9},{9,10},{10,1... | collective-permute-start | bytes 1572872 | tf_op jit(solution)/shard_map/ppermute | solution.py:25
  96.1 11.8 %collective-permute-start.13 = (f32[512,256]{1,0:T(8,128)S(1)}, f32[512,256]{1,0:T(8,128)S(1)}, u32[]{:S(2)}, u32[]{:S(2)}) collective-permute-start(f32[512,256]{1,0:T(8,128)S(1)} %collective-permute-done.11), channel_id=1, source_target_pairs={{0,15},{1,0},{2,1},{3,2},{4,3},{5,4},{6,5},{7,6},{8,7},{9,8},{10,9... | collective-permute-start | bytes 1572872 | tf_op jit(solution)/shard_map/ppermute | solution.py:30
  103.4 11.3 %collective-permute-start.14 = (f32[512,256]{1,0:T(8,128)S(1)}, f32[512,256]{1,0:T(8,128)S(1)}, u32[]{:S(2)}, u32[]{:S(2)}) collective-permute-start(f32[512,256]{1,0:T(8,128)S(1)} %collective-permute-done.12), channel_id=1, source_target_pairs={{0,1},{1,2},{2,3},{3,4},{4,5},{5,6},{6,7},{7,8},{8,9},{9,10},{10,1... | collective-permute-start | bytes 1572872 | tf_op jit(solution)/shard_map/ppermute | solution.py:25
  132.2 158.2 %reduce-scatter.5.cloned.1.call-start = ((), (), s32[]{:S(2)}) async-start(), calls=%async_computation.3 | async-start | bytes 4456448 | tf_op jit(solution)/shard_map/reduce_scatter | solution.py:52
  137.7 12.3 %copy-start.4 = (f32[4,128,128]{2,1,0:T(8,128)S(1)}, f32[4,128,128]{2,1,0:T(8,128)}, u32[]{:S(2)}) copy-start(f32[4,128,128]{2,1,0:T(8,128)} %param.9) | copy-start | bytes 786436
  137.7 152.7 %copy-start.3 = (f32[512,128]{1,0:T(8,128)S(1)}, f32[512,128]{1,0:T(8,128)}, u32[]{:S(2)}) copy-start(f32[512,128]{1,0:T(8,128)} %param.8) | copy-start | bytes 786436
Sparse Core Ops, SparseCore 0:
  132.3 69.6 reduce-scatter.2
  204.6 62.5 reduce-scatter.4
